TPU v7x, 32 devices: a whole 2x2x4 slice. The times are simulated.
32 devices in a mesh: surf: 8 (over z, x), col: 4 (over y, core).
Axes of the slice: x: 2, y: 2, z: 4, core: 2. Of those that a mesh axis runs over, the one named last changes fastest.
Arguments:
- stiffness: float32 [32, 3, 512, 512], P(('surf', 'col'))
- load: float32 [32, 3, 512, 256], P(('surf', 'col')), may hold values from -6 to 6
- start: float32 [32, 3, 512, 256], P(('surf', 'col')), may hold values from -6 to 6
- boundary_matrix: float32 [512, 4, 2048], P('surf', None, 'col'), may hold values from -0.125 to 0.125
- bem_node: int32 [4, 512], P('col'), may hold values from 0 to 511, as said below
Outputs:
- solution_field: float32 [32, 3, 512, 256], P(('surf', 'col'))
- traction: float32 [4, 512, 256], P('col', 'surf')
Inputs may be any that keep to these rules, and one draw needn't show every extreme that they name: Each row bem_node[g] is a permutation of 0 to 512 - 1 (the top face nodes of column group g). For each block of 64 slots q in [s * 64, (s + 1) * 64) and each patch s2 of the group, the block's slots name either exactly 8 node of patch s2 or none; each patch's top face nodes lie in exactly 8 blocks.
All inputs are finite; a program needn't handle non-finite values.
Results may differ from a plain program's by a relative error of at most 0.0001.
Values sent between devices are 32-bit elements; how exact they have to be, the bound alone decides.
No kernel may reach another device: no remote copies, remote signals or barrier semaphores. Data moves between devices by JAX's collectives and lax.ppermute only.
A program may use at most 128 MiB of HBM per device.

v0:
```python
import jax
import jax.numpy as jnp
from jax import lax
from jax.sharding import PartitionSpec as P

EDGE = 8
ITERS = 2
damping = 0.25
coupling = 0.5


def with_halo(block, sides, width):
    for axis, dim in sides:
        count = lax.axis_size(axis)
        forward = [(i, i + 1) for i in range(count - 1)]
        backward = [(target, source) for source, target in forward]
        low = lax.ppermute(
            lax.slice_in_dim(block, block.shape[dim] - width, None, axis=dim), axis, forward
        )
        high = lax.ppermute(lax.slice_in_dim(block, 0, width, axis=dim), axis, backward)
        block = jnp.concatenate([low, block, high], axis=dim)
    return block


def volume_apply(current, kmats, edge_cells, layers_deep, fields):
    highest = lax.Precision.HIGHEST
    cube = current.reshape(layers_deep, edge_cells, edge_cells, edge_cells, fields)
    padded = with_halo(cube, (("surf", 1), ("col", 2)), 1)
    extra = jnp.zeros_like(cube)
    extra = extra.at[:, 0].add(cube[:, 0] - padded[:, 0, 1:-1])
    extra = extra.at[:, -1].add(cube[:, -1] - padded[:, -1, 1:-1])
    extra = extra.at[:, :, 0].add(cube[:, :, 0] - padded[:, 1:-1, 0])
    extra = extra.at[:, :, -1].add(cube[:, :, -1] - padded[:, 1:-1, -1])
    low_k = cube[:, :, :, 0]
    high_k = cube[:, :, :, -1]
    deeper = jnp.concatenate([low_k[1:], jnp.zeros_like(low_k[:1])], axis=0)
    extra = extra.at[:, :, :, -1].add(high_k - deeper)
    extra = extra.at[1:, :, :, 0].add(low_k[1:] - high_k[:-1])
    applied = jnp.einsum("dab,dbf->daf", kmats, current, precision=highest)
    return applied.reshape(cube.shape) + coupling * extra


def rank_within(labels_row, order_key):
    same_label = labels_row[:, None] == labels_row[None, :]
    earlier = order_key[None, :] < order_key[:, None]
    return jnp.sum(jnp.logical_and(same_label, earlier), axis=1)


def shards(stiffness, load, start, boundary_matrix, bem_node):
    highest = lax.Precision.HIGHEST
    surf_count = lax.axis_size("surf")
    my_index = lax.axis_index("surf")
    layers_deep = stiffness.shape[1]
    node_count = stiffness.shape[2]
    fields = load.shape[3]
    edge_cells = EDGE
    face_nodes = edge_cells * edge_cells
    per_pair = max(face_nodes // surf_count, 1)
    group_map = bem_node[0]
    group_size = group_map.shape[0]
    slot_of_node = jnp.argsort(group_map)
    kmats = stiffness[0]
    load_cube = load[0].reshape(layers_deep, edge_cells, edge_cells, edge_cells, fields)
    operator_rows = boundary_matrix.reshape(-1, group_size)
    local_order = jnp.arange(face_nodes, dtype=jnp.int32)
    my_block_nodes = lax.dynamic_slice_in_dim(group_map, my_index * face_nodes, face_nodes)
    block_owners = my_block_nodes // face_nodes
    block_local = my_block_nodes % face_nodes
    slot_index = block_owners * per_pair + rank_within(block_owners, block_local)
    my_node_slots = lax.dynamic_slice_in_dim(slot_of_node, my_index * face_nodes, face_nodes)
    node_holders = my_node_slots // face_nodes
    send_index = node_holders * per_pair + rank_within(node_holders, local_order)
    current = start[0]
    traction_rows = jnp.zeros((face_nodes, fields), jnp.float32)
    for turn_index in range(ITERS):
        cube = current.reshape(layers_deep, edge_cells, edge_cells, edge_cells, fields)
        top_face = cube[0, :, :, 0, :].reshape(face_nodes, fields)
        gathered = lax.all_gather(top_face, "surf", axis=0, tiled=True)
        ordered = jnp.take(gathered, group_map, axis=0)
        partial_value = jnp.dot(
            operator_rows, ordered, precision=highest, preferred_element_type=jnp.float32
        )
        summed = lax.psum_scatter(
            partial_value.reshape(face_nodes, -1, fields), "col", scatter_dimension=1, tiled=True
        )
        traction_rows = summed.reshape(face_nodes, fields)
        outgoing_back = (
            jnp.zeros((surf_count * per_pair, fields), jnp.float32)
            .at[slot_index]
            .set(traction_rows)
        )
        returned = lax.all_to_all(
            outgoing_back.reshape(surf_count, per_pair, fields),
            "surf",
            split_axis=0,
            concat_axis=0,
            tiled=True,
        )
        on_top = jnp.take(returned.reshape(surf_count * per_pair, fields), send_index, axis=0)
        applied = volume_apply(current, kmats, edge_cells, layers_deep, fields)
        applied = applied.at[0, :, :, 0, :].add(on_top.reshape(edge_cells, edge_cells, fields))
        residual = load_cube - applied
        current = (cube + damping * residual).reshape(layers_deep, node_count, fields)
    return (current[None], traction_rows[None])


def solution(mesh):
    in_specs = (
        P(("surf", "col"), None, None, None),
        P(("surf", "col"), None, None, None),
        P(("surf", "col"), None, None, None),
        P("surf", None, "col"),
        P("col", None),
    )
    out_specs = (P(("surf", "col"), None, None, None), P("col", "surf", None))
    return jax.shard_map(shards, mesh=mesh, in_specs=in_specs, out_specs=out_specs, check_vma=False)
```

profile of v0, /device:TPU:1, one launch (start us, length us, event | category | flops | bytes accessed | tf_op | source)
XLA Modules:
  0.0 254.0 jit_solution(10524862129218521562)
XLA Ops:
  11.2 4.6 %collective-permute-start = (f32[3,1,8,8,256]{4,2,1,0,3:T(8,128)}, f32[3,1,8,8,256]{4,2,1,0,3:T(8,128)}, u32[]{:S(2)}, u32[]{:S(2)}) collective-permute-start(f32[3,1,8,8,256]{4,2,1,0,3:T(8,128)} %slice.588), channel_id=1, source_target_pairs={{0,4},{4,8},{8,12},{12,16},{16,20},{20,24},{24,28},{1,5},{5,9},{9,... | collective-permute-start | bytes 589832 | tf_op jit(solution)/shard_map/ppermute | solution.py:17
  16.9 28.2 %all_gather.6 = f32[512,256]{1,0:T(8,128)} all-gather(f32[64,256]{1,0:T(8,128)S(1)} %bitcast.136), channel_id=1, replica_groups=mesh['surf'=8,'col'=4] {'surf'}, dimensions={0}, use_global_device_ids=true | all-gather | bytes 589824 | tf_op jit(solution)/shard_map/all_gather | solution.py:78
  47.2 3.3 %gather_fusion = f32[512,256]{1,0:T(8,128)} fusion(f32[512,256]{1,0:T(8,128)} %all_gather.6, s32[1024]{0:T(1024)S(1)} %pad_clamp_fusion.1), kind=kCustom, calls=%fused_computation.clone | custom fusion | bytes 1050624 | tf_op jit(solution)/shard_map/jit(_take)/gather | solution.py:79
  54.9 5.4 %fusion.2 = f32[3,512,256]{2,1,0:T(8,128)} fusion(f32[1,3,512,512]{3,2,1,0:T(8,128)S(1)} %copy-done, f32[1,3,512,256]{3,2,1,0:T(8,128)} %param.39), kind=kOutput, calls=%fused_computation.8 | convolution fusion | flops 2415919104 | bytes 6291456 | tf_op jit(solution)/shard_map/dab,dbf->daf/dot_general | solution.py:39
  60.4 3.8 %sort.17 = (s32[512]{0:T(512)}, s32[512]{0:T(512)S(1)}) sort(s32[512]{0:T(512)S(1)} %bitcast.141, s32[512]{0:T(512)S(1)} %iota.11), dimensions={0}, to_apply=%region_3.5 | sort | flops 4608 | bytes 8192 | tf_op jit(solution)/shard_map/jit(argsort)/sort | solution.py:61
  68.8 3.3 %collective-permute-done.1 = f32[3,1,8,8,256]{4,2,1,0,3:T(8,128)S(1)} collective-permute-done((f32[3,1,8,8,256]{4,2,1,0,3:T(8,128)S(1)}, f32[3,1,8,8,256]{4,2,1,0,3:T(8,128)S(1)}, u32[]{:S(2)}, u32[]{:S(2)}) %collective-permute-start.1) | collective-permute-done | bytes 196640 | tf_op jit(solution)/shard_map/ppermute | solution.py:20
  74.9 10.4 %collective-permute-start.2 = (f32[3,10,1,8,256]{4,2,1,0,3:T(1,128)}, f32[3,10,1,8,256]{4,2,1,0,3:T(1,128)}, u32[]{:S(2)}, u32[]{:S(2)}) collective-permute-start(f32[3,10,1,8,256]{4,2,1,0,3:T(1,128)} %get-tuple-element.181), channel_id=1, source_target_pairs={{0,1},{1,2},{2,3},{4,5},{5,6},{6,7},{8,9},{9,10},{10,11},{12,13},{... | collective-permute-start | bytes 737288 | tf_op jit(solution)/shard_map/ppermute | solution.py:17
  89.1 3.4 %all-to-all-start = ((f32[8,8,256]{2,1,0:T(8,128)}), f32[8,8,256]{2,1,0:T(8,128)S(1)}, u32[]{:S(2)}, u32[]{:S(2)}) async-start(f32[8,8,256]{2,1,0:T(8,128)} %bitcast.16), calls=%async_computation.1 | async-start | bytes 131072 | tf_op jit(solution)/shard_map/all_to_all | solution.py:92
  92.7 2.3 fusion.25
  95.0 4.5 %scatter-add.50 = f32[3,8,8,8,256]{4,2,1,0,3:T(8,128)} dynamic-update-slice(f32[3,8,8,8,256]{4,2,1,0,3:T(8,128)} %get-tuple-element.193, f32[3,8,1,8,256]{4,2,1,0,3:T(1,128)S(1)} %fusion.25, s32[]{:T(128)} %constant.397.clone.1, s32[]{:T(128)} %constant.397.clone.1, s32[]{:T(128)} %constant.397.clone.1, s32[]{:T(128)} %constant.397.clone.1, s32[]{:T(128)} %constant.397.clone.1) | dynamic-update-slice | bytes 393220 | tf_op jit(solution)/shard_map/scatter-add | solution.py:32
  99.5 2.4 fusion.24
  101.9 4.5 %scatter-add.51 = f32[3,8,8,8,256]{4,2,1,0,3:T(8,128)} dynamic-update-slice(f32[3,8,8,8,256]{4,2,1,0,3:T(8,128)} %scatter-add.50, f32[3,8,1,8,256]{4,2,1,0,3:T(1,128)S(1)} %fusion.24, s32[]{:T(128)} %constant.397.clone.1, s32[]{:T(128)} %constant.397.clone.1, s32[]{:T(128)} %constant.398.clone.1, s32[]{:T(128)} %constant.397.clone.1, s32[]{:T(128)} %constant.397.clone.1) | dynamic-update-slice | bytes 393220 | tf_op jit(solution)/shard_map/scatter-add | solution.py:33
  108.1 3.5 %copy.78 = f32[3,8,8,8,256]{4,3,2,1,0:T(8,128)} copy(f32[3,8,8,8,256]{4,2,1,0,3:T(8,128)} %fusion.23) | data formatting | bytes 3145728 | tf_op jit(solution)/shard_map/scatter-add | solution.py:37
  114.3 4.0 %scatter-add.55 = f32[3,8,8,8,256]{4,3,2,1,0:T(8,128)} dynamic-update-slice(f32[3,8,8,8,256]{4,3,2,1,0:T(8,128)} %copy.78, f32[2,8,8,1,256]{4,3,2,1,0:T(1,128)S(1)} %fusion.27, s32[]{:T(128)} %constant.399.clone.1, s32[]{:T(128)} %constant.397.clone.1, s32[]{:T(128)} %constant.397.clone.1, s32[]{:T(128)} %constant.397.clone.1, s32[]{:T(128)} %constant.397.clone.1) | dynamic-update-slice | bytes 262148 | tf_op jit(solution)/shard_map/scatter-add | solution.py:38
  118.3 3.3 %multiply_add_fusion.3 = f32[3,8,8,8,256]{4,3,2,1,0:T(8,128)} fusion(f32[3,8,8,8,256]{4,3,2,1,0:T(8,128)} %bitcast.130, f32[3,8,8,8,256]{4,3,2,1,0:T(8,128)} %scatter-add.55), kind=kLoop, calls=%fused_computation.14 | loop fusion | flops 786432 | bytes 4718592 | tf_op jit(solution)/shard_map/add | solution.py:40
  123.5 2.3 scatter-add.56
  125.8 2.8 %multiply_add_fusion.2 = f32[3,8,8,8,256]{4,3,2,1,0:T(8,128)S(1)} fusion(f32[3,8,8,8,256]{4,3,2,1,0:T(8,128)} %bitcast.124, f32[3,8,8,8,256]{4,3,2,1,0:T(8,128)} %bitcast.128, f32[3,8,8,8,256]{4,3,2,1,0:T(8,128)} %scatter-add.56), kind=kLoop, calls=%fused_computation.13 | loop fusion | flops 1179648 | bytes 6291456 | tf_op jit(solution)/shard_map/add | solution.py:103
  131.6 3.7 %collective-permute-start.4 = (f32[3,1,8,8,256]{4,2,1,0,3:T(8,128)}, f32[3,1,8,8,256]{4,2,1,0,3:T(8,128)}, u32[]{:S(2)}, u32[]{:S(2)}) collective-permute-start(f32[3,1,8,8,256]{4,2,1,0,3:T(8,128)} %slice.605), channel_id=1, source_target_pairs={{0,4},{4,8},{8,12},{12,16},{16,20},{20,24},{24,28},{1,5},{5,9},{9,... | collective-permute-start | bytes 589832 | tf_op jit(solution)/shard_map/ppermute | solution.py:17
  135.3 28.4 %all_gather.7 = f32[512,256]{1,0:T(8,128)} all-gather(f32[64,256]{1,0:T(8,128)S(1)} %bitcast.137), channel_id=1, replica_groups=mesh['surf'=8,'col'=4] {'surf'}, dimensions={0}, use_global_device_ids=true | all-gather | bytes 589824 | tf_op jit(solution)/shard_map/all_gather | solution.py:78
  163.7 3.3 %gather_fusion.2 = f32[512,256]{1,0:T(8,128)} fusion(f32[512,256]{1,0:T(8,128)} %all_gather.7, s32[1024]{0:T(1024)S(1)} %pad_clamp_fusion.1), kind=kCustom, calls=%fused_computation.2.clone | custom fusion | bytes 1050624 | tf_op jit(solution)/shard_map/jit(_take)/gather | solution.py:79
  175.8 4.6 %collective-permute-done.5 = f32[3,1,8,8,256]{4,2,1,0,3:T(8,128)S(1)} collective-permute-done((f32[3,1,8,8,256]{4,2,1,0,3:T(8,128)S(1)}, f32[3,1,8,8,256]{4,2,1,0,3:T(8,128)S(1)}, u32[]{:S(2)}, u32[]{:S(2)}) %collective-permute-start.5) | collective-permute-done | bytes 196640 | tf_op jit(solution)/shard_map/ppermute | solution.py:20
  183.2 10.5 %collective-permute-start.6 = (f32[3,10,1,8,256]{4,2,1,0,3:T(1,128)}, f32[3,10,1,8,256]{4,2,1,0,3:T(1,128)}, u32[]{:S(2)}, u32[]{:S(2)}) collective-permute-start(f32[3,10,1,8,256]{4,2,1,0,3:T(1,128)} %get-tuple-element.179), channel_id=1, source_target_pairs={{0,1},{1,2},{2,3},{4,5},{5,6},{6,7},{8,9},{9,10},{10,11},{12,13},{... | collective-permute-start | bytes 737288 | tf_op jit(solution)/shard_map/ppermute | solution.py:17
  193.7 6.5 %fusion.5 = f32[3,512,256]{1,2,0:T(8,128)} fusion(f32[3,512,256]{2,1,0:T(8,128)S(1)} %bitcast.120, f32[1,3,512,512]{3,2,1,0:T(8,128)S(1)} %copy-done), kind=kOutput, calls=%fused_computation.15 | convolution fusion | flops 2415919104 | bytes 6291456 | tf_op jit(solution)/shard_map/dab,dbf->daf/dot_general | solution.py:39
  200.3 3.0 %copy.82 = f32[3,512,256]{2,1,0:T(8,128)} copy(f32[3,512,256]{1,2,0:T(8,128)} %fusion.5) | data formatting | bytes 3145728 | tf_op jit(solution)/shard_map/dab,dbf->daf/dot_general | solution.py:39
  208.8 3.3 %all-to-all-start.1 = ((f32[8,8,256]{2,1,0:T(8,128)}), f32[8,8,256]{2,1,0:T(8,128)S(1)}, u32[]{:S(2)}, u32[]{:S(2)}) async-start(f32[8,8,256]{2,1,0:T(8,128)} %bitcast.26), calls=%async_computation.3 | async-start | bytes 131072 | tf_op jit(solution)/shard_map/all_to_all | solution.py:92
  214.0 4.5 %scatter-add.61 = f32[3,8,8,8,256]{4,2,1,0,3:T(8,128)} dynamic-update-slice(f32[3,8,8,8,256]{4,2,1,0,3:T(8,128)} %get-tuple-element.191, f32[3,8,1,8,256]{4,2,1,0,3:T(1,128)S(1)} %fusion.19, s32[]{:T(128)} %constant.397.clone.1, s32[]{:T(128)} %constant.397.clone.1, s32[]{:T(128)} %constant.397.clone.1, s32[]{:T(128)} %constant.397.clone.1, s32[]{:T(128)} %constant.397.clone.1) | dynamic-update-slice | bytes 393220 | tf_op jit(solution)/shard_map/scatter-add | solution.py:32
  220.4 4.5 %scatter-add.64 = f32[3,8,8,8,256]{4,2,1,0,3:T(8,128)} dynamic-update-slice(f32[3,8,8,8,256]{4,2,1,0,3:T(8,128)} %scatter-add.61, f32[3,8,1,8,256]{4,2,1,0,3:T(1,128)S(1)} %fusion.18, s32[]{:T(128)} %constant.397.clone.1, s32[]{:T(128)} %constant.397.clone.1, s32[]{:T(128)} %constant.398.clone.1, s32[]{:T(128)} %constant.397.clone.1, s32[]{:T(128)} %constant.397.clone.1) | dynamic-update-slice | bytes 393220 | tf_op jit(solution)/shard_map/scatter-add | solution.py:33
  229.3 3.5 %copy.90 = f32[3,8,8,8,256]{4,3,2,1,0:T(8,128)} copy(f32[3,8,8,8,256]{4,2,1,0,3:T(8,128)} %fusion.17) | data formatting | bytes 3145728 | tf_op jit(solution)/shard_map/scatter-add | solution.py:37
  233.5 4.0 %scatter-add.66 = f32[3,8,8,8,256]{4,3,2,1,0:T(8,128)} dynamic-update-slice(f32[3,8,8,8,256]{4,3,2,1,0:T(8,128)} %copy.90, f32[2,8,8,1,256]{4,3,2,1,0:T(1,128)S(1)} %fusion.26, s32[]{:T(128)} %constant.399.clone.1, s32[]{:T(128)} %constant.397.clone.1, s32[]{:T(128)} %constant.397.clone.1, s32[]{:T(128)} %constant.397.clone.1, s32[]{:T(128)} %constant.397.clone.1) | dynamic-update-slice | bytes 262148 | tf_op jit(solution)/shard_map/scatter-add | solution.py:38
  237.5 2.1 multiply_add_fusion.1
  240.9 2.3 scatter-add.69
  243.2 3.9 %multiply_add_fusion = f32[3,8,8,8,256]{4,3,2,1,0:T(8,128)} fusion(f32[3,8,8,8,256]{4,3,2,1,0:T(8,128)} %copy-done.1, f32[3,8,8,8,256]{4,3,2,1,0:T(8,128)} %bitcast.129, f32[3,8,8,8,256]{4,3,2,1,0:T(8,128)} %scatter-add.69), kind=kLoop, calls=%fused_computation.11 | loop fusion | flops 1179648 | bytes 6291456 | tf_op jit(solution)/shard_map/add | solution.py:103
  (94 shorter events, 59.4 us)
Async XLA Ops:
  7.2 47.8 %copy-start = (f32[1,3,512,512]{3,2,1,0:T(8,128)S(1)}, f32[1,3,512,512]{3,2,1,0:T(8,128)}, u32[]{:S(2)}) copy-start(f32[1,3,512,512]{3,2,1,0:T(8,128)} %param.37) | copy-start | bytes 9437188
  7.2 80.2 %reduce-scatter.3.cloned.1.call-start = ((), (), s32[]{:S(2)}) async-start(), calls=%async_computation.4 | async-start | bytes 327680 | tf_op jit(solution)/shard_map/reduce_scatter | solution.py:83
  7.2 9.6 %copy-start.7 = (s32[1,512]{1,0:T(1,128)S(1)}, s32[1,512]{1,0:T(1,128)}, u32[]{:S(2)}) copy-start(s32[1,512]{1,0:T(1,128)} %param.41) | copy-start | bytes 6148
  9.3 1.2 copy-start.5
  11.2 53.5 %collective-permute-start = (f32[3,1,8,8,256]{4,2,1,0,3:T(8,128)}, f32[3,1,8,8,256]{4,2,1,0,3:T(8,128)}, u32[]{:S(2)}, u32[]{:S(2)}) collective-permute-start(f32[3,1,8,8,256]{4,2,1,0,3:T(8,128)} %slice.588), channel_id=1, source_target_pairs={{0,4},{4,8},{8,12},{12,16},{16,20},{20,24},{24,28},{1,5},{5,9},{9,... | collective-permute-start | bytes 589832 | tf_op jit(solution)/shard_map/ppermute | solution.py:17
  64.2 4.2 %copy-start.3 = (f32[1,3,512,256]{3,2,1,0:T(8,128)S(1)}, f32[1,3,512,256]{3,2,1,0:T(8,128)}, u32[]{:S(2)}) copy-start(f32[1,3,512,256]{3,2,1,0:T(8,128)} %param.39) | copy-start | bytes 4718596
  65.8 6.4 %collective-permute-start.1 = (f32[3,1,8,8,256]{4,2,1,0,3:T(8,128)S(1)}, f32[3,1,8,8,256]{4,2,1,0,3:T(8,128)S(1)}, u32[]{:S(2)}, u32[]{:S(2)}) collective-permute-start(f32[3,1,8,8,256]{4,2,1,0,3:T(8,128)S(1)} %get-tuple-element.186), channel_id=1, source_target_pairs={{4,0},{8,4},{12,8},{16,12},{20,16},{24,20},{28,24},{5,1},{9,5},{13... | collective-permute-start | bytes 589832 | tf_op jit(solution)/shard_map/ppermute | solution.py:20
  74.9 17.8 %collective-permute-start.2 = (f32[3,10,1,8,256]{4,2,1,0,3:T(1,128)}, f32[3,10,1,8,256]{4,2,1,0,3:T(1,128)}, u32[]{:S(2)}, u32[]{:S(2)}) collective-permute-start(f32[3,10,1,8,256]{4,2,1,0,3:T(1,128)} %get-tuple-element.181), channel_id=1, source_target_pairs={{0,1},{1,2},{2,3},{4,5},{5,6},{6,7},{8,9},{9,10},{10,11},{12,13},{... | collective-permute-start | bytes 737288 | tf_op jit(solution)/shard_map/ppermute | solution.py:17
  85.5 3.7 %copy-start.8 = (s32[64]{0:T(128)}, s32[64]{0:T(128)S(1)}, u32[]{:S(2)}) copy-start(s32[64]{0:T(128)S(1)} %fusion.36) | copy-start | bytes 772
  85.5 14.0 %collective-permute-start.3 = (f32[3,10,1,8,256]{4,2,1,0,3:T(1,128)}, f32[3,10,1,8,256]{4,2,1,0,3:T(1,128)}, u32[]{:S(2)}, u32[]{:S(2)}) collective-permute-start(f32[3,10,1,8,256]{4,2,1,0,3:T(1,128)} %get-tuple-element.180), channel_id=1, source_target_pairs={{1,0},{2,1},{3,2},{5,4},{6,5},{7,6},{9,8},{10,9},{11,10},{13,12},{... | collective-permute-start | bytes 737288 | tf_op jit(solution)/shard_map/ppermute | solution.py:20
  89.1 32.5 %all-to-all-start = ((f32[8,8,256]{2,1,0:T(8,128)}), f32[8,8,256]{2,1,0:T(8,128)S(1)}, u32[]{:S(2)}, u32[]{:S(2)}) async-start(f32[8,8,256]{2,1,0:T(8,128)} %bitcast.16), calls=%async_computation.1 | async-start | bytes 131072 | tf_op jit(solution)/shard_map/all_to_all | solution.py:92
  92.5 114.6 %reduce-scatter.5.cloned.1.call-start = ((), (), s32[]{:S(2)}) async-start(), calls=%async_computation.5 | async-start | bytes 327680 | tf_op jit(solution)/shard_map/reduce_scatter | solution.py:83
  128.6 1.1 copy-start.1
  129.7 1.2 copy-start.6
  131.6 39.9 %collective-permute-start.4 = (f32[3,1,8,8,256]{4,2,1,0,3:T(8,128)}, f32[3,1,8,8,256]{4,2,1,0,3:T(8,128)}, u32[]{:S(2)}, u32[]{:S(2)}) collective-permute-start(f32[3,1,8,8,256]{4,2,1,0,3:T(8,128)} %slice.605), channel_id=1, source_target_pairs={{0,4},{4,8},{8,12},{12,16},{16,20},{20,24},{24,28},{1,5},{5,9},{9,... | collective-permute-start | bytes 589832 | tf_op jit(solution)/shard_map/ppermute | solution.py:17
  171.4 3.9 %copy-start.2 = (f32[3,8,8,8,256]{4,3,2,1,0:T(8,128)S(1)}, f32[3,8,8,8,256]{4,3,2,1,0:T(8,128)}, u32[]{:S(2)}) copy-start(f32[3,8,8,8,256]{4,3,2,1,0:T(8,128)} %copy-done.1) | copy-start | bytes 4718596
  174.0 6.4 %collective-permute-start.5 = (f32[3,1,8,8,256]{4,2,1,0,3:T(8,128)S(1)}, f32[3,1,8,8,256]{4,2,1,0,3:T(8,128)S(1)}, u32[]{:S(2)}, u32[]{:S(2)}) collective-permute-start(f32[3,1,8,8,256]{4,2,1,0,3:T(8,128)S(1)} %get-tuple-element.184), channel_id=1, source_target_pairs={{4,0},{8,4},{12,8},{16,12},{20,16},{24,20},{28,24},{5,1},{9,5},{13... | collective-permute-start | bytes 589832 | tf_op jit(solution)/shard_map/ppermute | solution.py:20
  183.2 28.9 %collective-permute-start.6 = (f32[3,10,1,8,256]{4,2,1,0,3:T(1,128)}, f32[3,10,1,8,256]{4,2,1,0,3:T(1,128)}, u32[]{:S(2)}, u32[]{:S(2)}) collective-permute-start(f32[3,10,1,8,256]{4,2,1,0,3:T(1,128)} %get-tuple-element.179), channel_id=1, source_target_pairs={{0,1},{1,2},{2,3},{4,5},{5,6},{6,7},{8,9},{9,10},{10,11},{12,13},{... | collective-permute-start | bytes 737288 | tf_op jit(solution)/shard_map/ppermute | solution.py:17
  205.1 13.3 %collective-permute-start.7 = (f32[3,10,1,8,256]{4,2,1,0,3:T(1,128)}, f32[3,10,1,8,256]{4,2,1,0,3:T(1,128)}, u32[]{:S(2)}, u32[]{:S(2)}) collective-permute-start(f32[3,10,1,8,256]{4,2,1,0,3:T(1,128)} %get-tuple-element.178), channel_id=1, source_target_pairs={{1,0},{2,1},{3,2},{5,4},{6,5},{7,6},{9,8},{10,9},{11,10},{13,12},{... | collective-permute-start | bytes 737288 | tf_op jit(solution)/shard_map/ppermute | solution.py:20
  208.8 24.0 %all-to-all-start.1 = ((f32[8,8,256]{2,1,0:T(8,128)}), f32[8,8,256]{2,1,0:T(8,128)S(1)}, u32[]{:S(2)}, u32[]{:S(2)}) async-start(f32[8,8,256]{2,1,0:T(8,128)} %bitcast.26), calls=%async_computation.3 | async-start | bytes 131072 | tf_op jit(solution)/shard_map/all_to_all | solution.py:92
  239.6 1.2 copy-start.4
Sparse Core Ops, SparseCore 0:
  55.0 24.3 reduce-scatter.2
  171.5 24.3 reduce-scatter.4
where the time goes:
time: 256 us; the launch traced here: 254 us
  local copies, waits for them, and re-layouts  77.7 us (30%)
  blocking collectives  56.6 us (22%)
  starting transfers between devices  42.6 us (17%)
  other arithmetic  38.9 us (15%)
  matrix products  15.7 us (6%)
  between operations  14.4 us (6%)
  waiting for transfers between devices  8.06 us (3%)
    all_gather x2, blocking collectives, shards(): gathered = lax.all_gather(top_face, 'surf', axis=0, tiled=True)  56.6 us
    ppermute x4, starting transfers between devices, with_halo(): lax.ppermute(lax.slice_in_dim(block, block.shape[dim] - width, None, axis...  29.2 us
    dot_general x2, matrix products, volume_apply(): applied = jnp.einsum('dab,dbf->daf', kmats, current, precision=highest)  11.9 us
    scatter-add x2, local copies, waits for them, and re-layouts, volume_apply(): extra = extra.at[:, :, 0].add(cube[:, :, 0] - padded[:, 1:-1, 0])  8.99 us
    scatter-add x2, local copies, waits for them, and re-layouts, volume_apply(): extra = extra.at[:, :, -1].add(cube[:, :, -1] - padded[:, 1:-1, -1])  8.99 us
    scatter-add x2, local copies, waits for them, and re-layouts, volume_apply(): extra = extra.at[1:, :, :, 0].add(low_k[1:] - high_k[:-1])  8 us
    ppermute x4, waiting for transfers between devices, with_halo(): lax.ppermute(lax.slice_in_dim(block, 0, width, axis=dim), axis, backward)  7.97 us
    scatter-add x2, local copies, waits for them, and re-layouts, volume_apply(): extra = extra.at[:, :, :, -1].add(high_k - deeper)  6.98 us
  transfers between devices with their start and end apart: 12, of which 2 were waited for; matrix products, arithmetic and copies ran while one was open for 41% of the time, Pallas kernels for 0%

commit v1 on v0

--- a/solution.py
+++ b/solution.py
@@ -75,7 +75,14 @@
     for turn_index in range(ITERS):
         cube = current.reshape(layers_deep, edge_cells, edge_cells, edge_cells, fields)
         top_face = cube[0, :, :, 0, :].reshape(face_nodes, fields)
-        gathered = lax.all_gather(top_face, "surf", axis=0, tiled=True)
+        ring = [top_face]
+        for hop in range(7):
+            ring.append(lax.ppermute(ring[-1], "surf", [(dev, (dev + 1) % 8) for dev in range(8)]))
+        gathered = jnp.roll(
+            jnp.concatenate(ring[::-1], axis=0),
+            (lax.axis_index("surf") + 1) * ring[0].shape[0],
+            axis=0,
+        )
         ordered = jnp.take(gathered, group_map, axis=0)
         partial_value = jnp.dot(
             operator_rows, ordered, precision=highest, preferred_element_type=jnp.float32

time: 256 us -> 242 us (0.945)
  blocking collectives: 56.6 us -> 0 us
  waiting for transfers between devices: 8.06 us -> 35 us
  starting transfers between devices: 42.6 us -> 51.1 us
  other arithmetic: 38.9 us -> 44.8 us
    all_gather x2 -> x0, blocking collectives: 56.6 us -> none  [shards(): gathered = lax.all_gather(top_face, 'surf', axis=0, tiled=True)]
    ppermute x0 -> x14, waiting for transfers between devices: none -> 30.1 us  [shards(): lax.ppermute(ring[-1], 'surf', [(dev, (dev + 1) % 8) for dev in range(8)])]
    ppermute x4, waiting for transfers between devices: 7.97 us -> 0.01 us  [with_halo(): lax.ppermute(lax.slice_in_dim(block, 0, width, axis=dim), axis, backward)]
    all_to_all x2, waiting for transfers between devices: 0.01 us -> 4.85 us  [shards(): lax.all_to_all(outgoing_back.reshape(surf_count, per_pair, fields), 'surf...]
    all_to_all x2, starting transfers between devices: 6.7 us -> 11.4 us  [shards(): lax.all_to_all(outgoing_back.reshape(surf_count, per_pair, fields), 'surf...]
    unnamed x24 -> x38, local copies, waits for them, and re-layouts: 5.05 us -> 8.53 us
    ppermute x0 -> x14, starting transfers between devices: none -> 3.17 us  [shards(): lax.ppermute(ring[-1], 'surf', [(dev, (dev + 1) % 8) for dev in range(8)])]
  transfers between devices with their start and end apart: 12 -> 26, of which waited for: 2 -> 12; matrix products, arithmetic and copies ran while one was open for 41% -> 48% of each run, Pallas kernels for 0% -> 0%
where the time goes in v1:
time: 242 us; the launch traced here: 239 us
  local copies, waits for them, and re-layouts  79.6 us (33%)
  starting transfers between devices  51.1 us (21%)
  other arithmetic  44.8 us (19%)
  waiting for transfers between devices  35 us (14%)
  between operations  14.5 us (6%)
  matrix products  14.3 us (6%)
    ppermute x14, waiting for transfers between devices, shards(): lax.ppermute(ring[-1], 'surf', [(dev, (dev + 1) % 8) for dev in range(8)])  30.1 us
    ppermute x4, starting transfers between devices, with_halo(): lax.ppermute(lax.slice_in_dim(block, block.shape[dim] - width, None, axis...  29.6 us
    all_to_all x2, starting transfers between devices, shards(): lax.all_to_all(outgoing_back.reshape(surf_count, per_pair, fields), 'surf...  11.4 us
    dot_general x2, matrix products, volume_apply(): applied = jnp.einsum('dab,dbf->daf', kmats, current, precision=highest)  10.5 us
    scatter-add x2, local copies, waits for them, and re-layouts, volume_apply(): extra = extra.at[:, :, -1].add(cube[:, :, -1] - padded[:, 1:-1, -1])  9 us
    scatter-add x2, local copies, waits for them, and re-layouts, volume_apply(): extra = extra.at[:, :, 0].add(cube[:, :, 0] - padded[:, 1:-1, 0])  8.99 us
    unnamed x38, local copies, waits for them, and re-layouts  8.53 us
    scatter-add x2, local copies, waits for them, and re-layouts, volume_apply(): extra = extra.at[1:, :, :, 0].add(low_k[1:] - high_k[:-1])  7.98 us
  transfers between devices with their start and end apart: 26, of which 12 were waited for; matrix products, arithmetic and copies ran while one was open for 48% of the time, Pallas kernels for 0%

profile of v1, /device:TPU:1, one launch (start us, length us, event | category | flops | bytes accessed | tf_op | source)
XLA Modules:
  0.0 239.3 jit_solution(15394127891354084897)
XLA Ops:
  11.2 4.6 %collective-permute-start = (f32[3,1,8,8,256]{4,2,1,0,3:T(8,128)}, f32[3,1,8,8,256]{4,2,1,0,3:T(8,128)}, u32[]{:S(2)}, u32[]{:S(2)}) collective-permute-start(f32[3,1,8,8,256]{4,2,1,0,3:T(8,128)} %slice.588), channel_id=1, source_target_pairs={{0,4},{4,8},{8,12},{12,16},{16,20},{20,24},{24,28},{1,5},{5,9},{9,... | collective-permute-start | bytes 589832 | tf_op jit(solution)/shard_map/ppermute | solution.py:17
  16.5 4.0 %fusion.2 = f32[3,512,256]{2,1,0:T(8,128)} fusion(f32[1,3,512,512]{3,2,1,0:T(8,128)S(1)} %copy-done, f32[1,3,512,256]{3,2,1,0:T(8,128)S(1)} %copy-done.2), kind=kOutput, calls=%fused_computation.8 | convolution fusion | flops 2415919104 | bytes 6291456 | tf_op jit(solution)/shard_map/dab,dbf->daf/dot_general | solution.py:39
  20.6 3.8 %sort.17 = (s32[512]{0:T(512)}, s32[512]{0:T(512)S(1)}) sort(s32[512]{0:T(512)S(1)} %bitcast.145, s32[512]{0:T(512)S(1)} %iota.11), dimensions={0}, to_apply=%region_3.6 | sort | flops 4608 | bytes 8192 | tf_op jit(solution)/shard_map/jit(argsort)/sort | solution.py:61
  31.8 5.5 %collective-permute-done.6 = f32[64,256]{1,0:T(8,128)S(1)} collective-permute-done((f32[64,256]{1,0:T(8,128)}, f32[64,256]{1,0:T(8,128)S(1)}, u32[]{:S(2)}, u32[]{:S(2)}) %collective-permute-start.6) | collective-permute-done | bytes 65568 | tf_op jit(solution)/shard_map/ppermute | solution.py:80
  37.9 5.2 %collective-permute-done.7 = f32[64,256]{1,0:T(8,128)S(1)} collective-permute-done((f32[64,256]{1,0:T(8,128)S(1)}, f32[64,256]{1,0:T(8,128)S(1)}, u32[]{:S(2)}, u32[]{:S(2)}) %collective-permute-start.7) | collective-permute-done | bytes 65568 | tf_op jit(solution)/shard_map/ppermute | solution.py:80
  45.5 3.5 %collective-permute-done.8 = f32[64,256]{1,0:T(8,128)S(1)} collective-permute-done((f32[64,256]{1,0:T(8,128)S(1)}, f32[64,256]{1,0:T(8,128)S(1)}, u32[]{:S(2)}, u32[]{:S(2)}) %collective-permute-start.8) | collective-permute-done | bytes 65568 | tf_op jit(solution)/shard_map/ppermute | solution.py:80
  52.2 2.7 %collective-permute-done.9 = f32[64,256]{1,0:T(8,128)S(1)} collective-permute-done((f32[64,256]{1,0:T(8,128)S(1)}, f32[64,256]{1,0:T(8,128)S(1)}, u32[]{:S(2)}, u32[]{:S(2)}) %collective-permute-start.9) | collective-permute-done | bytes 65568 | tf_op jit(solution)/shard_map/ppermute | solution.py:80
  57.7 10.2 %collective-permute-start.2 = (f32[3,10,1,8,256]{4,2,1,0,3:T(1,128)}, f32[3,10,1,8,256]{4,2,1,0,3:T(1,128)}, u32[]{:S(2)}, u32[]{:S(2)}) collective-permute-start(f32[3,10,1,8,256]{4,2,1,0,3:T(1,128)} %get-tuple-element.182), channel_id=1, source_target_pairs={{0,1},{1,2},{2,3},{4,5},{5,6},{6,7},{8,9},{9,10},{10,11},{12,13},{... | collective-permute-start | bytes 737288 | tf_op jit(solution)/shard_map/ppermute | solution.py:17
  72.0 3.3 %gather_fusion = f32[512,256]{1,0:T(8,128)} fusion(f32[512,256]{1,0:T(8,128)} %fusion.9, s32[1024]{0:T(1024)S(1)} %pad_clamp_fusion.1), kind=kCustom, calls=%fused_computation.clone | custom fusion | bytes 1050624 | tf_op jit(solution)/shard_map/jit(_take)/gather | solution.py:86
  82.0 4.5 %scatter-add.50 = f32[3,8,8,8,256]{4,2,1,0,3:T(8,128)} dynamic-update-slice(f32[3,8,8,8,256]{4,2,1,0,3:T(8,128)} %get-tuple-element.194, f32[3,8,1,8,256]{4,2,1,0,3:T(1,128)S(1)} %fusion.27, s32[]{:T(128)} %constant.415.clone.1, s32[]{:T(128)} %constant.415.clone.1, s32[]{:T(128)} %constant.415.clone.1, s32[]{:T(128)} %constant.415.clone.1, s32[]{:T(128)} %constant.415.clone.1) | dynamic-update-slice | bytes 393220 | tf_op jit(solution)/shard_map/scatter-add | solution.py:32
  88.9 4.5 %scatter-add.51 = f32[3,8,8,8,256]{4,2,1,0,3:T(8,128)} dynamic-update-slice(f32[3,8,8,8,256]{4,2,1,0,3:T(8,128)} %scatter-add.50, f32[3,8,1,8,256]{4,2,1,0,3:T(1,128)S(1)} %fusion.26, s32[]{:T(128)} %constant.415.clone.1, s32[]{:T(128)} %constant.415.clone.1, s32[]{:T(128)} %constant.416.clone.1, s32[]{:T(128)} %constant.415.clone.1, s32[]{:T(128)} %constant.415.clone.1) | dynamic-update-slice | bytes 393220 | tf_op jit(solution)/shard_map/scatter-add | solution.py:33
  95.1 3.5 %copy.78 = f32[3,8,8,8,256]{4,3,2,1,0:T(8,128)} copy(f32[3,8,8,8,256]{4,2,1,0,3:T(8,128)} %fusion.25) | data formatting | bytes 3145728 | tf_op jit(solution)/shard_map/scatter-add | solution.py:37
  101.4 4.0 %scatter-add.55 = f32[3,8,8,8,256]{4,3,2,1,0:T(8,128)} dynamic-update-slice(f32[3,8,8,8,256]{4,3,2,1,0:T(8,128)} %copy.78, f32[2,8,8,1,256]{4,3,2,1,0:T(1,128)S(1)} %fusion.29, s32[]{:T(128)} %constant.417.clone.1, s32[]{:T(128)} %constant.415.clone.1, s32[]{:T(128)} %constant.415.clone.1, s32[]{:T(128)} %constant.415.clone.1, s32[]{:T(128)} %constant.415.clone.1) | dynamic-update-slice | bytes 262148 | tf_op jit(solution)/shard_map/scatter-add | solution.py:38
  107.0 5.7 %all-to-all-start = ((f32[8,8,256]{2,1,0:T(8,128)}), f32[8,8,256]{2,1,0:T(8,128)S(1)}, u32[]{:S(2)}, u32[]{:S(2)}) async-start(f32[8,8,256]{2,1,0:T(8,128)} %bitcast.16), calls=%async_computation.1 | async-start | bytes 131072 | tf_op jit(solution)/shard_map/all_to_all | solution.py:99
  112.8 3.3 %multiply_add_fusion.3 = f32[3,8,8,8,256]{4,3,2,1,0:T(8,128)} fusion(f32[3,8,8,8,256]{4,3,2,1,0:T(8,128)} %bitcast.134, f32[3,8,8,8,256]{4,3,2,1,0:T(8,128)} %scatter-add.55), kind=kLoop, calls=%fused_computation.14 | loop fusion | flops 786432 | bytes 4718592 | tf_op jit(solution)/shard_map/add | solution.py:40
  122.7 2.8 %multiply_add_fusion.2 = f32[3,8,8,8,256]{4,3,2,1,0:T(8,128)S(1)} fusion(f32[3,8,8,8,256]{4,3,2,1,0:T(8,128)} %bitcast.129, f32[3,8,8,8,256]{4,3,2,1,0:T(8,128)} %bitcast.132, f32[3,8,8,8,256]{4,3,2,1,0:T(8,128)} %scatter-add.56), kind=kLoop, calls=%fused_computation.13 | loop fusion | flops 1179648 | bytes 6291456 | tf_op jit(solution)/shard_map/add | solution.py:110
  127.3 3.6 %collective-permute-start.11 = (f32[3,1,8,8,256]{4,2,1,0,3:T(8,128)S(1)}, f32[3,1,8,8,256]{4,2,1,0,3:T(8,128)}, u32[]{:S(2)}, u32[]{:S(2)}) collective-permute-start(f32[3,1,8,8,256]{4,2,1,0,3:T(8,128)S(1)} %slice.605), channel_id=1, source_target_pairs={{0,4},{4,8},{8,12},{12,16},{16,20},{20,24},{24,28},{1,5},{5,9},{9,... | collective-permute-start | bytes 589832 | tf_op jit(solution)/shard_map/ppermute | solution.py:17
  132.2 6.5 %fusion.5 = f32[3,512,256]{1,2,0:T(8,128)} fusion(f32[3,512,256]{2,1,0:T(8,128)S(1)} %bitcast.124, f32[1,3,512,512]{3,2,1,0:T(8,128)S(1)} %copy-done), kind=kOutput, calls=%fused_computation.15 | convolution fusion | flops 2415919104 | bytes 6291456 | tf_op jit(solution)/shard_map/dab,dbf->daf/dot_general | solution.py:39
  140.4 3.1 %copy.82 = f32[3,512,256]{2,1,0:T(8,128)} copy(f32[3,512,256]{1,2,0:T(8,128)} %fusion.5) | data formatting | bytes 3145728 | tf_op jit(solution)/shard_map/dab,dbf->daf/dot_general | solution.py:39
  147.1 3.7 %collective-permute-done.18 = f32[64,256]{1,0:T(8,128)S(1)} collective-permute-done((f32[64,256]{1,0:T(8,128)}, f32[64,256]{1,0:T(8,128)S(1)}, u32[]{:S(2)}, u32[]{:S(2)}) %collective-permute-start.18) | collective-permute-done | bytes 65568 | tf_op jit(solution)/shard_map/ppermute | solution.py:80
  154.0 2.6 %collective-permute-done.19 = f32[64,256]{1,0:T(8,128)S(1)} collective-permute-done((f32[64,256]{1,0:T(8,128)S(1)}, f32[64,256]{1,0:T(8,128)S(1)}, u32[]{:S(2)}, u32[]{:S(2)}) %collective-permute-start.19) | collective-permute-done | bytes 65568 | tf_op jit(solution)/shard_map/ppermute | solution.py:80
  158.7 3.7 %collective-permute-done.20 = f32[64,256]{1,0:T(8,128)S(1)} collective-permute-done((f32[64,256]{1,0:T(8,128)S(1)}, f32[64,256]{1,0:T(8,128)S(1)}, u32[]{:S(2)}, u32[]{:S(2)}) %collective-permute-start.20) | collective-permute-done | bytes 65568 | tf_op jit(solution)/shard_map/ppermute | solution.py:80
  163.5 11.2 %collective-permute-start.13 = (f32[3,10,1,8,256]{4,2,1,0,3:T(1,128)}, f32[3,10,1,8,256]{4,2,1,0,3:T(1,128)}, u32[]{:S(2)}, u32[]{:S(2)}) collective-permute-start(f32[3,10,1,8,256]{4,2,1,0,3:T(1,128)} %get-tuple-element.180), channel_id=1, source_target_pairs={{0,1},{1,2},{2,3},{4,5},{5,6},{6,7},{8,9},{9,10},{10,11},{12,13},{... | collective-permute-start | bytes 737288 | tf_op jit(solution)/shard_map/ppermute | solution.py:17
  178.8 3.3 %gather_fusion.2 = f32[512,256]{1,0:T(8,128)} fusion(f32[512,256]{1,0:T(8,128)} %fusion.8, s32[1024]{0:T(1024)S(1)} %pad_clamp_fusion.1), kind=kCustom, calls=%fused_computation.2.clone | custom fusion | bytes 1050624 | tf_op jit(solution)/shard_map/jit(_take)/gather | solution.py:86
  188.3 4.5 %scatter-add.61 = f32[3,8,8,8,256]{4,2,1,0,3:T(8,128)} dynamic-update-slice(f32[3,8,8,8,256]{4,2,1,0,3:T(8,128)} %get-tuple-element.192, f32[3,8,1,8,256]{4,2,1,0,3:T(1,128)S(1)} %fusion.21, s32[]{:T(128)} %constant.415.clone.1, s32[]{:T(128)} %constant.415.clone.1, s32[]{:T(128)} %constant.415.clone.1, s32[]{:T(128)} %constant.415.clone.1, s32[]{:T(128)} %constant.415.clone.1) | dynamic-update-slice | bytes 393220 | tf_op jit(solution)/shard_map/scatter-add | solution.py:32
  194.7 4.5 %scatter-add.64 = f32[3,8,8,8,256]{4,2,1,0,3:T(8,128)} dynamic-update-slice(f32[3,8,8,8,256]{4,2,1,0,3:T(8,128)} %scatter-add.61, f32[3,8,1,8,256]{4,2,1,0,3:T(1,128)S(1)} %fusion.20, s32[]{:T(128)} %constant.415.clone.1, s32[]{:T(128)} %constant.415.clone.1, s32[]{:T(128)} %constant.416.clone.1, s32[]{:T(128)} %constant.415.clone.1, s32[]{:T(128)} %constant.415.clone.1) | dynamic-update-slice | bytes 393220 | tf_op jit(solution)/shard_map/scatter-add | solution.py:33
  202.0 3.5 %copy.90 = f32[3,8,8,8,256]{4,3,2,1,0:T(8,128)} copy(f32[3,8,8,8,256]{4,2,1,0,3:T(8,128)} %fusion.19) | data formatting | bytes 3145728 | tf_op jit(solution)/shard_map/scatter-add | solution.py:37
  207.2 4.0 %scatter-add.66 = f32[3,8,8,8,256]{4,3,2,1,0:T(8,128)} dynamic-update-slice(f32[3,8,8,8,256]{4,3,2,1,0:T(8,128)} %copy.90, f32[2,8,8,1,256]{4,3,2,1,0:T(1,128)S(1)} %fusion.28, s32[]{:T(128)} %constant.417.clone.1, s32[]{:T(128)} %constant.415.clone.1, s32[]{:T(128)} %constant.415.clone.1, s32[]{:T(128)} %constant.415.clone.1, s32[]{:T(128)} %constant.415.clone.1) | dynamic-update-slice | bytes 262148 | tf_op jit(solution)/shard_map/scatter-add | solution.py:38
  212.9 5.7 %all-to-all-start.1 = ((f32[8,8,256]{2,1,0:T(8,128)}), f32[8,8,256]{2,1,0:T(8,128)S(1)}, u32[]{:S(2)}, u32[]{:S(2)}) async-start(f32[8,8,256]{2,1,0:T(8,128)} %bitcast.26), calls=%async_computation.3 | async-start | bytes 131072 | tf_op jit(solution)/shard_map/all_to_all | solution.py:99
  218.6 3.3 %multiply_add_fusion.1 = f32[3,8,8,8,256]{4,3,2,1,0:T(8,128)} fusion(f32[3,8,8,8,256]{4,3,2,1,0:T(8,128)} %bitcast.131, f32[3,8,8,8,256]{4,3,2,1,0:T(8,128)} %scatter-add.66), kind=kLoop, calls=%fused_computation.12 | loop fusion | flops 786432 | bytes 4718592 | tf_op jit(solution)/shard_map/add | solution.py:40
  221.9 2.4 %all-to-all-done.1 = f32[8,8,256]{2,1,0:T(8,128)S(1)} async-done(((f32[8,8,256]{2,1,0:T(8,128)}), f32[8,8,256]{2,1,0:T(8,128)S(1)}, u32[]{:S(2)}, u32[]{:S(2)}) %all-to-all-start.1) | async-done | bytes 65568 | tf_op jit(solution)/shard_map/all_to_all | solution.py:99
  228.5 3.9 %multiply_add_fusion = f32[3,8,8,8,256]{4,3,2,1,0:T(8,128)} fusion(f32[3,8,8,8,256]{4,3,2,1,0:T(8,128)} %copy-done.1, f32[3,8,8,8,256]{4,3,2,1,0:T(8,128)} %bitcast.133, f32[3,8,8,8,256]{4,3,2,1,0:T(8,128)} %scatter-add.69), kind=kLoop, calls=%fused_computation.11 | loop fusion | flops 1179648 | bytes 6291456 | tf_op jit(solution)/shard_map/add | solution.py:110
  (138 shorter events, 84.5 us)
Async XLA Ops:
  7.2 9.3 %copy-start = (f32[1,3,512,512]{3,2,1,0:T(8,128)S(1)}, f32[1,3,512,512]{3,2,1,0:T(8,128)}, u32[]{:S(2)}) copy-start(f32[1,3,512,512]{3,2,1,0:T(8,128)} %param.39) | copy-start | bytes 9437188
  7.2 98.1 %reduce-scatter.3.cloned.1.call-start = ((), (), s32[]{:S(2)}) async-start(), calls=%async_computation.4 | async-start | bytes 327680 | tf_op jit(solution)/shard_map/reduce_scatter | solution.py:90
  7.2 8.6 %copy-start.2 = (f32[1,3,512,256]{3,2,1,0:T(8,128)S(1)}, f32[1,3,512,256]{3,2,1,0:T(8,128)}, u32[]{:S(2)}) copy-start(f32[1,3,512,256]{3,2,1,0:T(8,128)} %param.41) | copy-start | bytes 4718596
  7.2 9.3 %copy-start.8 = (s32[1,512]{1,0:T(1,128)S(1)}, s32[1,512]{1,0:T(1,128)}, u32[]{:S(2)}) copy-start(s32[1,512]{1,0:T(1,128)} %param.43) | copy-start | bytes 6148
  11.2 32.0 %collective-permute-start = (f32[3,1,8,8,256]{4,2,1,0,3:T(8,128)}, f32[3,1,8,8,256]{4,2,1,0,3:T(8,128)}, u32[]{:S(2)}, u32[]{:S(2)}) collective-permute-start(f32[3,1,8,8,256]{4,2,1,0,3:T(8,128)} %slice.588), channel_id=1, source_target_pairs={{0,4},{4,8},{8,12},{12,16},{16,20},{20,24},{24,28},{1,5},{5,9},{9,... | collective-permute-start | bytes 589832 | tf_op jit(solution)/shard_map/ppermute | solution.py:17
  15.8 9.5 %collective-permute-start.4 = (f32[64,256]{1,0:T(8,128)S(1)}, f32[64,256]{1,0:T(8,128)S(1)}, u32[]{:S(2)}, u32[]{:S(2)}) collective-permute-start(f32[64,256]{1,0:T(8,128)S(1)} %bitcast.141), channel_id=1, source_target_pairs={{0,4},{4,8},{8,12},{12,16},{16,20},{20,24},{24,28},{28,0},{1,5},{5... | collective-permute-start | bytes 196616 | tf_op jit(solution)/shard_map/ppermute | solution.py:80
  25.3 18.9 %copy-start.6 = (f32[64,256]{1,0:T(8,128)}, f32[64,256]{1,0:T(8,128)S(1)}, u32[]{:S(2)}) copy-start(f32[64,256]{1,0:T(8,128)S(1)} %collective-permute-done.4) | copy-start | bytes 196612
  25.3 6.0 %collective-permute-start.5 = (f32[64,256]{1,0:T(8,128)S(1)}, f32[64,256]{1,0:T(8,128)}, u32[]{:S(2)}, u32[]{:S(2)}) collective-permute-start(f32[64,256]{1,0:T(8,128)S(1)} %collective-permute-done.4), channel_id=1, source_target_pairs={{0,4},{4,8},{8,12},{12,16},{16,20},{20,24},{24,28},{28,0},{1,5},{5... | collective-permute-start | bytes 196616 | tf_op jit(solution)/shard_map/ppermute | solution.py:80
  31.3 6.0 %collective-permute-start.6 = (f32[64,256]{1,0:T(8,128)}, f32[64,256]{1,0:T(8,128)S(1)}, u32[]{:S(2)}, u32[]{:S(2)}) collective-permute-start(f32[64,256]{1,0:T(8,128)} %collective-permute-done.5), channel_id=1, source_target_pairs={{0,4},{4,8},{8,12},{12,16},{16,20},{20,24},{24,28},{28,0},{1,5},{5... | collective-permute-start | bytes 196616 | tf_op jit(solution)/shard_map/ppermute | solution.py:80
  37.3 5.8 %collective-permute-start.7 = (f32[64,256]{1,0:T(8,128)S(1)}, f32[64,256]{1,0:T(8,128)S(1)}, u32[]{:S(2)}, u32[]{:S(2)}) collective-permute-start(f32[64,256]{1,0:T(8,128)S(1)} %collective-permute-done.6), channel_id=1, source_target_pairs={{0,4},{4,8},{8,12},{12,16},{16,20},{20,24},{24,28},{28,0},{1,5},{5... | collective-permute-start | bytes 196616 | tf_op jit(solution)/shard_map/ppermute | solution.py:80
  43.1 5.9 %collective-permute-start.8 = (f32[64,256]{1,0:T(8,128)S(1)}, f32[64,256]{1,0:T(8,128)S(1)}, u32[]{:S(2)}, u32[]{:S(2)}) collective-permute-start(f32[64,256]{1,0:T(8,128)S(1)} %collective-permute-done.7), channel_id=1, source_target_pairs={{0,4},{4,8},{8,12},{12,16},{16,20},{20,24},{24,28},{28,0},{1,5},{5... | collective-permute-start | bytes 196616 | tf_op jit(solution)/shard_map/ppermute | solution.py:80
  44.2 10.7 %collective-permute-start.1 = (f32[3,1,8,8,256]{4,2,1,0,3:T(8,128)S(1)}, f32[3,1,8,8,256]{4,2,1,0,3:T(8,128)S(1)}, u32[]{:S(2)}, u32[]{:S(2)}) collective-permute-start(f32[3,1,8,8,256]{4,2,1,0,3:T(8,128)S(1)} %get-tuple-element.187), channel_id=1, source_target_pairs={{4,0},{8,4},{12,8},{16,12},{20,16},{24,20},{28,24},{5,1},{9,5},{13... | collective-permute-start | bytes 589832 | tf_op jit(solution)/shard_map/ppermute | solution.py:20
  49.0 5.9 %collective-permute-start.9 = (f32[64,256]{1,0:T(8,128)S(1)}, f32[64,256]{1,0:T(8,128)S(1)}, u32[]{:S(2)}, u32[]{:S(2)}) collective-permute-start(f32[64,256]{1,0:T(8,128)S(1)} %collective-permute-done.8), channel_id=1, source_target_pairs={{0,4},{4,8},{8,12},{12,16},{16,20},{20,24},{24,28},{28,0},{1,5},{5... | collective-permute-start | bytes 196616 | tf_op jit(solution)/shard_map/ppermute | solution.py:80
  52.2 18.8 %copy-start.7 = (f32[64,256]{1,0:T(8,128)S(1)}, f32[64,256]{1,0:T(8,128)}, u32[]{:S(2)}) copy-start(f32[64,256]{1,0:T(8,128)} %copy-done.6) | copy-start | bytes 196612
  54.9 15.1 %collective-permute-start.10 = (f32[64,256]{1,0:T(8,128)S(1)}, f32[64,256]{1,0:T(8,128)S(1)}, u32[]{:S(2)}, u32[]{:S(2)}) collective-permute-start(f32[64,256]{1,0:T(8,128)S(1)} %collective-permute-done.9), channel_id=1, source_target_pairs={{0,4},{4,8},{8,12},{12,16},{16,20},{20,24},{24,28},{28,0},{1,5},{5... | collective-permute-start | bytes 196616 | tf_op jit(solution)/shard_map/ppermute | solution.py:80
  57.7 22.0 %collective-permute-start.2 = (f32[3,10,1,8,256]{4,2,1,0,3:T(1,128)}, f32[3,10,1,8,256]{4,2,1,0,3:T(1,128)}, u32[]{:S(2)}, u32[]{:S(2)}) collective-permute-start(f32[3,10,1,8,256]{4,2,1,0,3:T(1,128)} %get-tuple-element.182), channel_id=1, source_target_pairs={{0,1},{1,2},{2,3},{4,5},{5,6},{6,7},{8,9},{9,10},{10,11},{12,13},{... | collective-permute-start | bytes 737288 | tf_op jit(solution)/shard_map/ppermute | solution.py:17
  67.9 18.6 %collective-permute-start.3 = (f32[3,10,1,8,256]{4,2,1,0,3:T(1,128)}, f32[3,10,1,8,256]{4,2,1,0,3:T(1,128)}, u32[]{:S(2)}, u32[]{:S(2)}) collective-permute-start(f32[3,10,1,8,256]{4,2,1,0,3:T(1,128)} %get-tuple-element.181), channel_id=1, source_target_pairs={{1,0},{2,1},{3,2},{5,4},{6,5},{7,6},{9,8},{10,9},{11,10},{13,12},{... | collective-permute-start | bytes 737288 | tf_op jit(solution)/shard_map/ppermute | solution.py:20
  107.0 11.5 %all-to-all-start = ((f32[8,8,256]{2,1,0:T(8,128)}), f32[8,8,256]{2,1,0:T(8,128)S(1)}, u32[]{:S(2)}, u32[]{:S(2)}) async-start(f32[8,8,256]{2,1,0:T(8,128)} %bitcast.16), calls=%async_computation.1 | async-start | bytes 131072 | tf_op jit(solution)/shard_map/all_to_all | solution.py:99
  112.7 98.5 %reduce-scatter.5.cloned.1.call-start = ((), (), s32[]{:S(2)}) async-start(), calls=%async_computation.5 | async-start | bytes 327680 | tf_op jit(solution)/shard_map/reduce_scatter | solution.py:90
  125.4 14.2 %copy-start.1 = (f32[3,8,8,8,256]{4,3,2,1,0:T(8,128)}, f32[3,8,8,8,256]{4,3,2,1,0:T(8,128)S(1)}, u32[]{:S(2)}) copy-start(f32[3,8,8,8,256]{4,3,2,1,0:T(8,128)S(1)} %multiply_add_fusion.2) | copy-start | bytes 4718596
  125.5 6.7 %collective-permute-start.15 = (f32[64,256]{1,0:T(8,128)S(1)}, f32[64,256]{1,0:T(8,128)S(1)}, u32[]{:S(2)}, u32[]{:S(2)}) collective-permute-start(f32[64,256]{1,0:T(8,128)S(1)} %bitcast.142), channel_id=1, source_target_pairs={{0,4},{4,8},{8,12},{12,16},{16,20},{20,24},{24,28},{28,0},{1,5},{5... | collective-permute-start | bytes 196616 | tf_op jit(solution)/shard_map/ppermute | solution.py:80
  127.3 17.3 %collective-permute-start.11 = (f32[3,1,8,8,256]{4,2,1,0,3:T(8,128)S(1)}, f32[3,1,8,8,256]{4,2,1,0,3:T(8,128)}, u32[]{:S(2)}, u32[]{:S(2)}) collective-permute-start(f32[3,1,8,8,256]{4,2,1,0,3:T(8,128)S(1)} %slice.605), channel_id=1, source_target_pairs={{0,4},{4,8},{8,12},{12,16},{16,20},{20,24},{24,28},{1,5},{5,9},{9,... | collective-permute-start | bytes 589832 | tf_op jit(solution)/shard_map/ppermute | solution.py:17
  132.2 6.5 %collective-permute-start.16 = (f32[64,256]{1,0:T(8,128)S(1)}, f32[64,256]{1,0:T(8,128)S(1)}, u32[]{:S(2)}, u32[]{:S(2)}) collective-permute-start(f32[64,256]{1,0:T(8,128)S(1)} %collective-permute-done.15), channel_id=1, source_target_pairs={{0,4},{4,8},{8,12},{12,16},{16,20},{20,24},{24,28},{28,0},{1,5},{5... | collective-permute-start | bytes 196616 | tf_op jit(solution)/shard_map/ppermute | solution.py:80
  138.7 5.9 %collective-permute-start.17 = (f32[64,256]{1,0:T(8,128)S(1)}, f32[64,256]{1,0:T(8,128)}, u32[]{:S(2)}, u32[]{:S(2)}) collective-permute-start(f32[64,256]{1,0:T(8,128)S(1)} %collective-permute-done.16), channel_id=1, source_target_pairs={{0,4},{4,8},{8,12},{12,16},{16,20},{20,24},{24,28},{28,0},{1,5},{5... | collective-permute-start | bytes 196616 | tf_op jit(solution)/shard_map/ppermute | solution.py:80
  144.7 6.1 %collective-permute-start.18 = (f32[64,256]{1,0:T(8,128)}, f32[64,256]{1,0:T(8,128)S(1)}, u32[]{:S(2)}, u32[]{:S(2)}) collective-permute-start(f32[64,256]{1,0:T(8,128)} %collective-permute-done.17), channel_id=1, source_target_pairs={{0,4},{4,8},{8,12},{12,16},{16,20},{20,24},{24,28},{28,0},{1,5},{5... | collective-permute-start | bytes 196616 | tf_op jit(solution)/shard_map/ppermute | solution.py:80
  145.8 11.3 %collective-permute-start.12 = (f32[3,1,8,8,256]{4,2,1,0,3:T(8,128)S(1)}, f32[3,1,8,8,256]{4,2,1,0,3:T(8,128)S(1)}, u32[]{:S(2)}, u32[]{:S(2)}) collective-permute-start(f32[3,1,8,8,256]{4,2,1,0,3:T(8,128)S(1)} %get-tuple-element.185), channel_id=1, source_target_pairs={{4,0},{8,4},{12,8},{16,12},{20,16},{24,20},{28,24},{5,1},{9,5},{13... | collective-permute-start | bytes 589832 | tf_op jit(solution)/shard_map/ppermute | solution.py:20
  150.8 5.8 %collective-permute-start.19 = (f32[64,256]{1,0:T(8,128)S(1)}, f32[64,256]{1,0:T(8,128)S(1)}, u32[]{:S(2)}, u32[]{:S(2)}) collective-permute-start(f32[64,256]{1,0:T(8,128)S(1)} %collective-permute-done.18), channel_id=1, source_target_pairs={{0,4},{4,8},{8,12},{12,16},{16,20},{20,24},{24,28},{28,0},{1,5},{5... | collective-permute-start | bytes 196616 | tf_op jit(solution)/shard_map/ppermute | solution.py:80
  156.6 5.8 %collective-permute-start.20 = (f32[64,256]{1,0:T(8,128)S(1)}, f32[64,256]{1,0:T(8,128)S(1)}, u32[]{:S(2)}, u32[]{:S(2)}) collective-permute-start(f32[64,256]{1,0:T(8,128)S(1)} %collective-permute-done.19), channel_id=1, source_target_pairs={{0,4},{4,8},{8,12},{12,16},{16,20},{20,24},{24,28},{28,0},{1,5},{5... | collective-permute-start | bytes 196616 | tf_op jit(solution)/shard_map/ppermute | solution.py:80
  162.4 14.4 %collective-permute-start.21 = (f32[64,256]{1,0:T(8,128)S(1)}, f32[64,256]{1,0:T(8,128)S(1)}, u32[]{:S(2)}, u32[]{:S(2)}) collective-permute-start(f32[64,256]{1,0:T(8,128)S(1)} %collective-permute-done.20), channel_id=1, source_target_pairs={{0,4},{4,8},{8,12},{12,16},{16,20},{20,24},{24,28},{28,0},{1,5},{5... | collective-permute-start | bytes 196616 | tf_op jit(solution)/shard_map/ppermute | solution.py:80
  163.5 23.0 %collective-permute-start.13 = (f32[3,10,1,8,256]{4,2,1,0,3:T(1,128)}, f32[3,10,1,8,256]{4,2,1,0,3:T(1,128)}, u32[]{:S(2)}, u32[]{:S(2)}) collective-permute-start(f32[3,10,1,8,256]{4,2,1,0,3:T(1,128)} %get-tuple-element.180), channel_id=1, source_target_pairs={{0,1},{1,2},{2,3},{4,5},{5,6},{6,7},{8,9},{9,10},{10,11},{12,13},{... | collective-permute-start | bytes 737288 | tf_op jit(solution)/shard_map/ppermute | solution.py:17
  174.6 18.2 %collective-permute-start.14 = (f32[3,10,1,8,256]{4,2,1,0,3:T(1,128)}, f32[3,10,1,8,256]{4,2,1,0,3:T(1,128)}, u32[]{:S(2)}, u32[]{:S(2)}) collective-permute-start(f32[3,10,1,8,256]{4,2,1,0,3:T(1,128)} %get-tuple-element.179), channel_id=1, source_target_pairs={{1,0},{2,1},{3,2},{5,4},{6,5},{7,6},{9,8},{10,9},{11,10},{13,12},{... | collective-permute-start | bytes 737288 | tf_op jit(solution)/shard_map/ppermute | solution.py:20
  212.9 11.5 %all-to-all-start.1 = ((f32[8,8,256]{2,1,0:T(8,128)}), f32[8,8,256]{2,1,0:T(8,128)S(1)}, u32[]{:S(2)}, u32[]{:S(2)}) async-start(f32[8,8,256]{2,1,0:T(8,128)} %bitcast.26), calls=%async_computation.3 | async-start | bytes 131072 | tf_op jit(solution)/shard_map/all_to_all | solution.py:99
  (3 other events, 10.4 us)
Sparse Core Ops, SparseCore 0:
  79.8 21.2 reduce-scatter.2
  186.6 21.2 reduce-scatter.4
